TPU v7x, 32 devices: a whole 2x2x4 slice. The times are simulated.
32 devices in a mesh: tm: 4 (over y, x), space: 8 (over z, core).
Axes of the slice: x: 2, y: 2, z: 4, core: 2. Of those that a mesh axis runs over, the one named last changes fastest.
Arguments:
- forcing: float32 [4, 64, 16384], P('tm', 'space'), may hold values from -6 to 6
- conductivity: float32 [64, 16384], P('space'), may hold values from 0.1 to 1
Outputs:
- solution: float32 [4, 64, 16384], P('tm', 'space')
All inputs are finite; a program needn't handle non-finite values.
Results may differ from a plain program's by a relative error of at most 0.0001.
Values sent between devices are 32-bit elements; how exact they have to be, the bound alone decides.
A program may use at most 64 MiB of HBM per device.

v0:
```python
import functools

import jax
import jax.numpy as jnp
from jax import lax
from jax.experimental import pallas as pl
from jax.experimental.pallas import tpu as pltpu
from jax.sharding import PartitionSpec as P

MESH = pl.DeviceIdType.MESH
LANES = 128
SUB = 8


def kernel(
    ntm, nsp, f_hbm, k_hbm, out_hbm,
    fstage, kloc, kstage, fwin, kwin, scl, inv, gn, gs, gw, ge, tau, abuf, bbuf, q0, q1, q2, res, part, red,
    f_sem, k_sem, r_sem, o_sem, own_sem,
):
    n = ntm * nsp
    mt, ms = lax.axis_index("tm"), lax.axis_index("space")
    me = mt * nsp + ms
    tl, _, own, rows, _ = f_hbm.shape
    steps, width = fwin.shape[0], fwin.shape[1]
    nx = scl.shape[1] - 2 * SUB
    blocks = nx // SUB

    def strip(s):
        return pl.ds(pl.multiple_of(SUB + s * rows, SUB), rows)

    def send(src, dst, sems, dt, ds):
        return pltpu.make_async_remote_copy(
            src_ref=src, dst_ref=dst, send_sem=sems.at[0], recv_sem=sems.at[1],
            device_id=(dt, ds), device_id_type=MESH)

    def f_copy(dt, ds):
        return send(fstage.at[:, dt * nsp + ds],
                    fwin.at[pl.ds(mt * tl, tl), :, strip(ms)], f_sem, dt, ds)

    def k_copy(dt, ds):
        return send(kstage.at[ds], kwin.at[:, strip(ms)], k_sem, dt, ds)

    def r_copy(dt, ds):
        return send(part, red.at[me], r_sem, dt, ds)

    def res_piece(dt, ds):
        return res.at[pl.ds(dt * tl, tl), :, pl.ds(pl.multiple_of(ds * rows, SUB), rows)]

    def o_copy(dt, ds):
        return send(res_piece(dt, ds), out_hbm.at[:, pl.ds(me * own, own)], o_sem, dt, ds)

    def await_bytes(ref, sem):
        pltpu.make_async_copy(ref, ref, sem).wait()

    def loop(low, high, act):
        def step(j, carry):
            act(j)
            return carry
        lax.fori_loop(low, high, step, 0)

    def turn(at, by, size):
        moved = at + by
        return jnp.where(moved >= size, moved - size, moved)

    def peers(act):
        for js in sorted(range(nsp), key=lambda j: abs(j - nsp // 2)):
            ds = turn(ms, js, nsp)
            for jt in range(ntm):
                if js or jt:
                    act(turn(mt, jt, ntm), ds)

    def side_peers(act):
        for js in range(1, nsp):
            act(mt, turn(ms, js, nsp))

    barrier = pltpu.get_barrier_semaphore()
    peers(lambda dt, ds: pl.semaphore_signal(
        barrier, inc=1, device_id=(dt, ds), device_id_type=MESH))
    loads = [
        pltpu.make_async_copy(f_hbm, fstage.at[:, :, pl.ds(0, own)], own_sem.at[0]),
        pltpu.make_async_copy(k_hbm, kloc, own_sem.at[1]),
        pltpu.make_async_copy(
            k_hbm.at[pl.ds(mt * nsp, nsp)], kstage.at[:, pl.ds(0, own)], own_sem.at[2]),
    ]
    for load in loads:
        load.start()
    zero = jnp.zeros((SUB, LANES), jnp.float32)
    for edge in (0, SUB + nx):
        for c in range(width):
            for ref in (kwin, scl):
                ref[c, edge:edge + SUB, :] = zero
            for ref in (tau, abuf, bbuf, q0, q1, q2):
                for s in range(steps):
                    ref[s, c, edge:edge + SUB, :] = zero
    lane = lax.broadcasted_iota(jnp.int32, (SUB, LANES), 1)
    first, last, ahead = lane == 0, lane == LANES - 1, lane < LANES // 2

    def beside(d, right, left):
        return jnp.where(ahead, right * jnp.where(d < n - 1, 1.0, 0.0),
                         left * jnp.where(d > 0, 1.0, 0.0))

    def after(d):
        return jnp.minimum(d + 1, n - 1)

    def before(d):
        return jnp.maximum(d - 1, 0)

    for load in loads:
        load.wait()

    def overlap_k(s):
        d = mt * nsp + s
        for r in range(0, rows, SUB):
            kstage[s, own, r:r + SUB, :] = beside(
                d, kloc[after(d), 0, r:r + SUB, :], kloc[before(d), own - 1, r:r + SUB, :])

    def overlap_f(d):
        for t in range(tl):
            for r in range(0, rows, SUB):
                fstage[t, d, own, r:r + SUB, :] = beside(
                    d, fstage[t, after(d), 0, r:r + SUB, :],
                    fstage[t, before(d), own - 1, r:r + SUB, :])

    loop(0, nsp, overlap_k)
    loop(0, n, overlap_f)
    own_k = pltpu.make_async_copy(kstage.at[ms], kwin.at[:, strip(ms)], k_sem.at[1])
    own_f = pltpu.make_async_copy(
        fstage.at[:, me], fwin.at[pl.ds(mt * tl, tl), :, strip(ms)], f_sem.at[1])
    pl.semaphore_wait(barrier, n - 1)

    side_peers(lambda dt, ds: k_copy(dt, ds).start())
    peers(lambda dt, ds: f_copy(dt, ds).start())
    own_k.start()
    own_f.start()
    await_bytes(kwin.at[:, pl.ds(SUB, nx)], k_sem.at[1])

    def lefts(xs):
        turned = [pltpu.roll(x, 1, 1) for x in xs]
        return [jnp.where(first, turned[c - 1], turned[c]) for c in range(width)]

    def rights(xs):
        turned = [pltpu.roll(x, LANES - 1, 1) for x in xs]
        return [jnp.where(last, turned[(c + 1) % width], turned[c]) for c in range(width)]

    def near(i, offset):
        return pl.ds(SUB + SUB * i + offset, SUB)

    def at(i):
        return pl.ds(pl.multiple_of(SUB + SUB * i, SUB), SUB)

    def flat(i):
        return pl.ds(pl.multiple_of(SUB * i, SUB), SUB)

    inside = beside(me, jnp.ones((SUB, LANES), jnp.float32), jnp.ones((SUB, LANES), jnp.float32))

    def weights_first(i):
        ks = [kwin[c, at(i), :] for c in range(width)]
        for c, (k, l, r) in enumerate(zip(ks, lefts(ks), rights(ks))):
            up, down = kwin[c, near(i, -1), :], kwin[c, near(i, 1), :]
            diag = 1.0 + 0.5 * (k + up) + 0.5 * (k + down) + 0.5 * (k + l) + 0.5 * (k + r)
            scale = 1.0 / jnp.sqrt(diag)
            scl[c, at(i), :] = scale * inside if c == own else scale
            inv[c, flat(i), :] = 1.0 / diag

    def weights_second(i):
        ks = [kwin[c, at(i), :] for c in range(width)]
        ss = [scl[c, at(i), :] for c in range(width)]
        quads = zip(ks, lefts(ks), rights(ks), ss, lefts(ss), rights(ss))
        for c, (k, kl, kr, s, sl, sr) in enumerate(quads):
            half = 0.5 * s
            gn[c, flat(i), :] = half * (k + kwin[c, near(i, -1), :]) * scl[c, near(i, -1), :]
            gs[c, flat(i), :] = half * (k + kwin[c, near(i, 1), :]) * scl[c, near(i, 1), :]
            gw[c, flat(i), :] = half * (k + kl) * sl
            ge[c, flat(i), :] = half * (k + kr) * sr

    loop(0, blocks, weights_first)
    loop(0, blocks, weights_second)

    await_bytes(fwin.at[:, :, pl.ds(SUB, nx)], f_sem.at[1])

    def scale_in(i):
        for c in range(width):
            s = scl[c, at(i), :]
            for t in range(steps):
                tau[t, c, at(i), :] = s * fwin[steps - 1 - t, c, at(i), :]

    loop(0, blocks, scale_in)

    def sweep(src, use):
        def block(i, total):
            xs, down, up = {}, {}, {}

            def fetch(c, t):
                if (c, t) not in xs:
                    x = src[t, c, at(i), :]
                    xs[c, t], down[c, t], up[c, t] = (
                        x, pltpu.roll(x, 1, 1), pltpu.roll(x, LANES - 1, 1))

            for c in range(width):
                wn, wso = gn[c, flat(i), :], gs[c, flat(i), :]
                ww, we = gw[c, flat(i), :], ge[c, flat(i), :]
                out = []
                for t in range(steps):
                    for b in (c - 1) % width, c, (c + 1) % width:
                        fetch(b, t)
                    left = jnp.where(first, down[(c - 1) % width, t], down[c, t])
                    right = jnp.where(last, up[(c + 1) % width, t], up[c, t])
                    out.append(
                        wn * src[t, c, near(i, -1), :] + wso * src[t, c, near(i, 1), :]
                        + (ww * left + we * right))
                term = use(c, i, [xs[c, t] for t in range(steps)], out)
                if term is not None and c < own:
                    total = total + term
            return total
        group = 8 if blocks % 8 == 0 else 1

        def several(i, total):
            for j in range(group):
                total = block(group * i + j, total)
            return total

        return lax.fori_loop(0, blocks // group, several, zero)

    def precondition(q):
        def one(c, i, x, g):
            for t in range(steps):
                abuf[t, c, at(i), :] = 0.5 * (x[t] + g[t])

        def two(c, i, x, g):
            for t in range(steps):
                bbuf[t, c, at(i), :] = 0.125 * tau[t, c, at(i), :] + g[t]

        def three(c, i, x, g):
            term = zero
            for t in range(steps):
                v = tau[t, c, at(i), :]
                y = 0.75 * v + g[t]
                q[t, c, at(i), :] = y
                term = term + v * y
            return term

        sweep(tau, one)
        sweep(abuf, two)
        return sweep(bbuf, three)

    def operate(q):
        def use(c, i, x, g):
            shrink = inv[c, flat(i), :]
            term = zero
            for t in range(steps):
                y = x[t] - g[t]
                if t:
                    y = y - shrink * x[t - 1]
                tau[steps - 1 - t, c, at(i), :] = y
                term = term + y * x[steps - 1 - t]
            return term
        return sweep(q, use)

    precondition(q0)
    m1 = operate(q0)
    m2 = precondition(q1)
    m3 = operate(q1)
    m4 = precondition(q2)
    m5 = operate(q2)

    def norm_one(c, i, x, g):
        term = zero
        for t in range(steps):
            abuf[t, c, at(i), :] = g[t]
            term = term + (x[t] * (0.75 * x[t] + 0.125 * g[t]) + 0.5 * (g[t] * g[t]))
        return term

    def norm_two(c, i, x, g):
        term = zero
        for t in range(steps):
            term = term + 0.5 * (x[t] * g[t])
        return term

    m6 = sweep(tau, norm_one) + sweep(abuf, norm_two)

    row = jnp.zeros((1, LANES), jnp.float32)
    lane1 = lax.broadcasted_iota(jnp.int32, (1, LANES), 1)
    for j, m in enumerate((m1, m2, m3, m4, m5, m6)):
        value = jnp.sum(jnp.sum(m, axis=0, keepdims=True), axis=1, keepdims=True)
        row = jnp.where(lane1 == j, value, row)
    part[...] = row
    red[me] = row
    peers(lambda dt, ds: r_copy(dt, ds).start())
    await_bytes(red.at[pl.ds(0, n - 1)], r_sem.at[1])
    total = lax.fori_loop(0, n, lambda j, acc: acc + red[j], jnp.zeros((1, LANES), jnp.float32))
    n1, n2, n3, n4, n5, n6 = [
        jnp.sum(jnp.where(lane1 == j, total, 0.0), axis=1, keepdims=True) for j in range(6)]

    tiny = 1e-7
    d1 = jnp.maximum(n2, 1e-37)
    l21, l31 = n3 / d1, n4 / d1
    d2 = jnp.maximum(n4 - l21 * n3, jnp.maximum(tiny * n4, 1e-37))
    e32 = n5 - l31 * n3
    l32 = e32 / d2
    d3 = jnp.maximum(n6 - l31 * n4 - l32 * e32, jnp.maximum(tiny * n6, 1e-37))
    y2 = n2 - l21 * n1
    y3 = n3 - l31 * n1 - l32 * y2
    a2 = y3 / d3
    a1 = y2 / d2 - l32 * a2
    a0 = n1 / d1 - l21 * a1 - l31 * a2

    def finish(i):
        for c in range(own):
            s = scl[c, at(i), :]
            s0, s1, s2 = a0 * s, a1 * s, a2 * s
            for t in range(steps):
                res[t, c, flat(i), :] = (
                    s0 * q0[t, c, at(i), :] + s1 * q1[t, c, at(i), :]
                    + s2 * q2[t, c, at(i), :])

    loop(0, blocks, finish)
    own_out = pltpu.make_async_copy(
        res_piece(mt, ms), out_hbm.at[:, pl.ds(me * own, own)], o_sem.at[1])
    own_out.start()
    peers(lambda dt, ds: o_copy(dt, ds).start())
    await_bytes(kstage.at[pl.ds(0, nsp - 1)], k_sem.at[0])
    await_bytes(fstage.at[:, pl.ds(0, n - 1)], f_sem.at[0])
    await_bytes(red.at[pl.ds(0, n - 1)], r_sem.at[0])
    await_bytes(out_hbm, o_sem.at[1])
    await_bytes(out_hbm.at[:, pl.ds(0, (n - 1) * own)], o_sem.at[0])


def solution(mesh):
    ntm, nsp = mesh.shape["tm"], mesh.shape["space"]
    n = ntm * nsp

    def body(forcing, conductivity):
        tl, rows, columns = forcing.shape
        tiles = columns // LANES
        own = tiles // n
        width = own + 1
        steps, nx = tl * ntm, rows * nsp
        f = forcing.reshape(tl, rows, n, own, LANES).transpose(0, 2, 3, 1, 4)
        k = conductivity.reshape(rows, n, own, LANES).transpose(1, 2, 0, 3)
        padded = pltpu.VMEM((width, nx + 2 * SUB, LANES), jnp.float32)
        plain = pltpu.VMEM((width, nx, LANES), jnp.float32)
        field = pltpu.VMEM((steps, width, nx + 2 * SUB, LANES), jnp.float32)
        dma = pltpu.SemaphoreType.DMA
        f, k = (pltpu.with_memory_space_constraint(x, pltpu.HBM) for x in (f, k))
        out = pl.pallas_call(
            functools.partial(kernel, ntm, nsp),
            out_shape=jax.ShapeDtypeStruct((tl, tiles, rows, LANES), jnp.float32),
            in_specs=[pl.BlockSpec(memory_space=pltpu.HBM)] * 2,
            out_specs=pl.BlockSpec(memory_space=pl.ANY),
            scratch_shapes=[
                pltpu.VMEM((tl, n, width, rows, LANES), jnp.float32),
                pltpu.VMEM((n, own, rows, LANES), jnp.float32),
                pltpu.VMEM((nsp, width, rows, LANES), jnp.float32),
                field, padded, padded, plain, plain, plain, plain, plain,
                field, field, field, field, field, field,
                pltpu.VMEM((steps, own, nx, LANES), jnp.float32),
                pltpu.VMEM((1, LANES), jnp.float32),
                pltpu.VMEM((n, 1, LANES), jnp.float32),
                dma((2,)), dma((2,)), dma((2,)), dma((2,)), dma((3,)),
            ],
            compiler_params=pltpu.CompilerParams(
                collective_id=0, has_side_effects=True, vmem_limit_bytes=24 * 1024 * 1024),
        )(f, k)
        return out.transpose(0, 2, 1, 3).reshape(tl, rows, columns)

    return jax.shard_map(
        body,
        mesh=mesh,
        in_specs=(P("tm", "space", None), P("space", None)),
        out_specs=P("tm", "space", None),
        check_vma=False,
    )
```

profile of v0, /device:TPU:1, one launch (start us, length us, event | category | flops | bytes accessed | tf_op | source)
XLA Modules:
  0.0 47.4 jit_solution(118528674227568364)
XLA Ops:
  0.0 46.6 %shard_map.28 = f32[1,128,8,128]{3,2,1,0:T(8,128)S(1)} custom-call(f32[1,32,4,8,128]{4,3,2,1,0:T(8,128)} %bitcast.10, f32[32,4,8,128]{3,2,1,0:T(8,128)} %bitcast.11), custom_call_target="tpu_custom_call" | custom-call | tf_op jit(solution)/shard_map/pallas_call | solution.py:345
  46.6 0.8 %copy.4 = f32[1,8,16384]{2,1,0:T(8,128)} copy(f32[1,8,16384]{2,1,0:T(8,128)S(1)} %bitcast.9) | data formatting | bytes 1048576
where the time goes:
time: 47.6 us; the launch traced here: 47.4 us
  Pallas kernels  46.6 us (98%)
  local copies, waits for them, and re-layouts  0.8 us (2%)
    pallas_call x1, Pallas kernels, body(): pl.pallas_call(functools.partial(kernel, ntm, nsp), out_shape=jax.ShapeDt...  46.6 us

commit v1 on v0

v1 whole, which is shorter than its diff:
```python
import functools

import jax
import jax.numpy as jnp
from jax import lax
from jax.experimental import pallas as pl
from jax.experimental.pallas import tpu as pltpu
from jax.sharding import PartitionSpec as P

MESH = pl.DeviceIdType.MESH
LANES = 128
SUB = 8
ITERS = 3
SWEEPS = 4 * ITERS + 2


def kernel(
    ntm, nsp, reach, f_hbm, k_hbm, out_hbm,
    fstage, kloc, kstage, fwin, kwin, scl, inv, gn, gs, gw, ge, taus, abufs, bbufs, qs, last, res, part, red,
    f_sem, k_sem, r_sem, o_sem, own_sem,
):
    n = ntm * nsp
    mt, ms = lax.axis_index("tm"), lax.axis_index("space")
    me = mt * nsp + ms
    tl, nb, own, rows, _ = f_hbm.shape
    steps, width = fwin.shape[0], fwin.shape[1]
    strips = nsp // 2
    half, ml = ms // strips, ms % strips
    mb = mt * strips + ml
    nx = scl.shape[1] - 2 * SUB
    groups, owned = nx // SUB, strips * rows // SUB
    spare = groups - owned
    edge = jnp.where(half == 0, ml >= strips - reach, ml < reach)

    def place(s, side):
        at = s - side * (strips - reach)
        return pl.ds(pl.multiple_of(SUB + at * rows, SUB), rows)

    def send(src, dst, sem, arrival, dt, ds):
        return pltpu.make_async_remote_copy(
            src_ref=src, dst_ref=dst, send_sem=sem, recv_sem=arrival,
            device_id=(dt, ds), device_id_type=MESH)

    def f_copy(dt, side, dl):
        return send(fstage.at[:, dt * strips + dl],
                    fwin.at[pl.ds(mt * tl, tl), :, place(ms, side)],
                    f_sem.at[0], f_sem.at[1], dt, side * strips + dl)

    def f_cross(dt, side, dl):
        return send(fstage.at[:, dt * strips + dl],
                    fwin.at[pl.ds(mt * tl, tl), :, place(ms, side)],
                    f_sem.at[0], f_sem.at[2], dt, side * strips + dl)

    def k_copy(side, dl):
        return send(kstage.at[dl], kwin.at[:, place(ms, side)],
                    k_sem.at[0], k_sem.at[1], mt, side * strips + dl)

    def r_copy(dt, ds):
        return send(part, red.at[me], r_sem.at[0], r_sem.at[1], dt, ds)

    def res_piece(dt, dl):
        return res.at[pl.ds(dt * tl, tl), :, pl.ds(pl.multiple_of(dl * rows, SUB), rows)]

    def o_copy(dt, dl):
        return send(res_piece(dt, dl), out_hbm.at[:, pl.ds(mb * own, own)],
                    o_sem.at[0], o_sem.at[1], dt, half * strips + dl)

    def await_bytes(ref, sem):
        pltpu.make_async_copy(ref, ref, sem).wait()

    def loop(low, high, act):
        def step(j, carry):
            act(j)
            return carry
        lax.fori_loop(low, high, step, 0)

    def turn(at, by, size):
        moved = at + by
        return jnp.where(moved >= size, moved - size, moved)

    def peers(act):
        for js in sorted(range(nsp), key=lambda j: abs(j - nsp // 2)):
            ds = turn(ms, js, nsp)
            for jt in range(ntm):
                if js or jt:
                    act(turn(mt, jt, ntm), ds)

    def home(i):
        return 2 * turn(ml // 2, 1 + i // 2, strips // 2) + (ml + i) % 2

    def mates(act):
        for i in range(strips):
            for jt in range(ntm):
                if (i, jt) != (strips - 2, 0):
                    act(turn(mt, jt, ntm), half, home(i))

    def across(i):
        near = 2 * (i // 2)
        return jnp.where(half == 0, near, strips - 2 - near) + (ml + i) % 2

    def others(act):
        for i in range(strips):
            for jt in range(ntm):
                act(turn(mt, jt, ntm), 1 - half, across(i))

    barrier = pltpu.get_barrier_semaphore()
    peers(lambda dt, ds: pl.semaphore_signal(
        barrier, inc=1, device_id=(dt, ds), device_id_type=MESH))
    loads = [
        pltpu.make_async_copy(f_hbm, fstage.at[:, :, pl.ds(0, own)], own_sem.at[0]),
        pltpu.make_async_copy(k_hbm, kloc, own_sem.at[1]),
        pltpu.make_async_copy(
            k_hbm.at[pl.ds(mt * strips, strips)], kstage.at[:, pl.ds(0, own)], own_sem.at[2]),
    ]
    for load in loads:
        load.start()
    lane = lax.broadcasted_iota(jnp.int32, (SUB, LANES), 1)
    first, final, ahead = lane == 0, lane == LANES - 1, lane < LANES // 2

    def beside(d, right, left):
        return jnp.where(ahead, right * jnp.where(d < nb - 1, 1.0, 0.0),
                         left * jnp.where(d > 0, 1.0, 0.0))

    def after(d):
        return jnp.minimum(d + 1, nb - 1)

    def before(d):
        return jnp.maximum(d - 1, 0)

    for load in loads:
        load.wait()

    def interleave(act):
        by = 1
        while by < own:
            odd = (lane & by) != 0

            def swap(tiles, by=by, odd=odd):
                pairs = [(c, c + by) for c in range(own) if not c & by]
                got = [[(get(a), get(b)) for a, b in pairs] for get, _ in tiles]
                turned = [[(pltpu.roll(y, by, 1), pltpu.roll(x, LANES - by, 1)) for x, y in g] for g in got]
                for (_, put), g, h in zip(tiles, got, turned):
                    for (a, b), (x, y), (ry, rx) in zip(pairs, g, h):
                        put(a, jnp.where(odd, ry, x))
                        put(b, jnp.where(odd, y, rx))

            act(swap, by == 1)
            by *= 2

    def overlap_k(s):
        d = mt * strips + s
        for r in range(0, rows, SUB):
            kstage[s, own, r:r + SUB, :] = beside(
                d, kloc[after(d), 0, r:r + SUB, :], kloc[before(d), own - 1, r:r + SUB, :])

    def overlap_f(d):
        for t in range(tl):
            for r in range(0, rows, SUB):
                fstage[t, d, own, r:r + SUB, :] = beside(
                    d, fstage[t, after(d), 0, r:r + SUB, :],
                    fstage[t, before(d), own - 1, r:r + SUB, :])

    def cell(ref, *head, r=0):
        def get(c):
            return ref[(*head, c, pl.ds(r, SUB), slice(None))]

        def put(c, x):
            ref[(*head, c, pl.ds(r, SUB), slice(None))] = x
        return get, put

    batch = 4 if nb % 4 == 0 else 1
    bands = range(0, rows, SUB)

    def weave_k(swap, _):
        swap([cell(kstage, s, r=r) for s in range(strips) for r in bands])

    def weave_f(swap, _):
        loop(0, nb // batch, lambda j: swap(
            [cell(fstage, t, batch * j + d, r=r) for d in range(batch) for t in range(tl) for r in bands]))

    loop(0, strips, overlap_k)
    interleave(weave_k)
    loop(0, nb, overlap_f)
    interleave(weave_f)
    own_k = pltpu.make_async_copy(kstage.at[ml], kwin.at[:, place(ms, half)], k_sem.at[1])
    own_f = pltpu.make_async_copy(
        fstage.at[:, mb], fwin.at[pl.ds(mt * tl, tl), :, place(ms, half)], f_sem.at[1])
    zero = jnp.zeros((SUB, LANES), jnp.float32)
    rims = (slice(0, SUB), slice(SUB + nx, SUB + nx + SUB))

    def clear(c):
        for rim in rims:
            kwin[c, rim, :] = zero
            scl[c, rim, :] = zero
            for s in range(steps):
                last[s, c, rim, :] = zero
                for many in (taus, abufs, bbufs, qs):
                    for j in range(many.shape[0]):
                        many[j, s, c, rim, :] = zero

    loop(0, width, clear)
    pl.semaphore_wait(barrier, n - 1)

    for i in range(strips):
        if i != strips - 2:
            k_copy(half, home(i)).start()

    @pl.when(edge)
    def _():
        for i in range(strips):
            k_copy(1 - half, across(i)).start()

    mates(lambda *to: f_copy(*to).start())

    @pl.when(edge)
    def _():
        others(lambda *to: f_cross(*to).start())

    own_k.start()
    own_f.start()
    await_bytes(kwin.at[:, pl.ds(SUB, nx)], k_sem.at[1])

    def turned(x0, x1, rim):
        down, up = pltpu.roll(rim, 1, 1), pltpu.roll(rim, LANES - 1, 1)
        start = jnp.where(lane < own, pltpu.roll(x1, own + 1, 1), pltpu.roll(x1, own, 1))
        end = jnp.where(lane >= LANES - own,
                        pltpu.roll(x0, LANES - own - 1, 1), pltpu.roll(x0, LANES - own, 1))
        return (jnp.where(first, down, start), jnp.where(first, pltpu.roll(x1, 1, 1), down),
                jnp.where(final, up, end), jnp.where(final, pltpu.roll(x0, LANES - 1, 1), up))

    def lefts(xs):
        ends = turned(xs[0], xs[own - 1], xs[own])
        return [ends[0], *xs[:own - 1], ends[1]]

    def rights(xs):
        ends = turned(xs[0], xs[own - 1], xs[own])
        return [*xs[1:own], ends[2], ends[3]]

    def near(i, offset):
        return pl.ds(SUB + SUB * i + offset, SUB)

    def at(i):
        return pl.ds(pl.multiple_of(SUB + SUB * i, SUB), SUB)

    def flat(i):
        return pl.ds(pl.multiple_of(SUB * i, SUB), SUB)

    inside = beside(mb, jnp.ones((SUB, LANES), jnp.float32), jnp.ones((SUB, LANES), jnp.float32))

    def weights_first(i):
        ks = [kwin[c, at(i), :] for c in range(width)]
        for c, (k, l, r) in enumerate(zip(ks, lefts(ks), rights(ks))):
            up, down = kwin[c, near(i, -1), :], kwin[c, near(i, 1), :]
            diag = 1.0 + 0.5 * (k + up) + 0.5 * (k + down) + 0.5 * (k + l) + 0.5 * (k + r)
            scale = 1.0 / jnp.sqrt(diag)
            scl[c, at(i), :] = scale * inside if c == own else scale
            inv[c, flat(i), :] = 1.0 / diag

    def weights_second(i):
        ks = [kwin[c, at(i), :] for c in range(width)]
        ss = [scl[c, at(i), :] for c in range(width)]
        quads = zip(ks, lefts(ks), rights(ks), ss, lefts(ss), rights(ss))
        for c, (k, kl, kr, s, sl, sr) in enumerate(quads):
            half_s = 0.5 * s
            gn[c, flat(i), :] = half_s * (k + kwin[c, near(i, -1), :]) * scl[c, near(i, -1), :]
            gs[c, flat(i), :] = half_s * (k + kwin[c, near(i, 1), :]) * scl[c, near(i, 1), :]
            gw[c, flat(i), :] = half_s * (k + kl) * sl
            ge[c, flat(i), :] = half_s * (k + kr) * sr

    loop(0, groups, weights_first)
    loop(0, groups, weights_second)

    def group(j):
        return jnp.where(half == 0, j, groups - 1 - j)

    def scale_in(j):
        i = group(j)
        for c in range(width):
            s = scl[c, at(i), :]
            for t in range(steps):
                taus[0, t, c, at(i), :] = s * fwin[steps - 1 - t, c, at(i), :]

    def sweep(src, use, low, high, total):
        def block(j, total):
            i = group(j)
            ends = []
            for t in range(steps):
                ends.append(turned(src[t, 0, at(i), :], src[t, own - 1, at(i), :], src[t, own, at(i), :]))

            def beside_of(t, c):
                here = ends[t]
                left = here[0] if c == 0 else here[1] if c == own else src[t, c - 1, at(i), :]
                right = here[2] if c == own - 1 else here[3] if c == own else src[t, c + 1, at(i), :]
                return left, right

            for c in (*range(1, own - 1), 0, own - 1, own):
                wn, wso = gn[c, flat(i), :], gs[c, flat(i), :]
                ww, we = gw[c, flat(i), :], ge[c, flat(i), :]
                out = []
                for t in range(steps):
                    left, right = beside_of(t, c)
                    out.append(
                        wn * src[t, c, near(i, -1), :] + wso * src[t, c, near(i, 1), :]
                        + (ww * left + we * right))
                term = use(c, i, [src[t, c, at(i), :] for t in range(steps)], out)
                if term is not None and c < own:
                    total = total + term
            return total
        return lax.fori_loop(low, high, block, total)

    def one(it):
        def use(c, i, x, g):
            for t in range(steps):
                abufs[it, t, c, at(i), :] = x[t] + g[t]
        return taus.at[it], use

    def two(it):
        def use(c, i, x, g):
            for t in range(steps):
                bbufs[it, t, c, at(i), :] = 0.25 * taus[it, t, c, at(i), :] + g[t]
        return abufs.at[it], use

    def three(it):
        def use(c, i, x, g):
            term = zero
            for t in range(steps):
                v = taus[it, t, c, at(i), :]
                y = 1.5 * v + g[t]
                qs[it, t, c, at(i), :] = y
                term = term + v * y
            return term
        return bbufs.at[it], use

    def operate(it):
        def use(c, i, x, g):
            shrink = inv[c, flat(i), :]
            term = zero
            for t in range(steps):
                y = x[t] - g[t]
                if t:
                    y = y - shrink * x[t - 1]
                taus[it + 1, steps - 1 - t, c, at(i), :] = y
                term = term + y * x[steps - 1 - t]
            return term
        return qs.at[it], use

    def norm_one(c, i, x, g):
        term = zero
        for t in range(steps):
            last[t, c, at(i), :] = g[t]
            term = term + (x[t] * (1.5 * x[t] + 0.25 * g[t]) + g[t] * g[t])
        return term

    def norm_two(c, i, x, g):
        term = zero
        for t in range(steps):
            term = term + x[t] * g[t]
        return term

    plan = []
    for it in range(ITERS):
        plan += [(*one(it), None), (*two(it), None),
                 (*three(it), 2 * it - 1 if it else None), (*operate(it), 2 * it)]
    plan += [(taus.at[ITERS], norm_one, 2 * ITERS - 1), (last, norm_two, 2 * ITERS - 1)]
    moments = [zero] * (2 * ITERS)

    def run(number, low, middle, high):
        src, use, slot = plan[number - 1]
        if low < middle:
            base = zero if slot is None else moments[slot]
            total = sweep(src, use, low, middle, base)
            if slot is not None:
                moments[slot] = total
        if max(low, middle) < high:
            sweep(src, use, max(low, middle), high, zero)

    def up_to(count):
        return -(-count // SUB)

    inner = owned * SUB
    ready = [(inner - j) // SUB for j in range(SWEEPS + 1)]
    early = [max(up_to(SUB * ready[i] + i - j) for i in range(j, SWEEPS + 1))
             for j in range(SWEEPS + 1)]
    need = [owned + up_to(SWEEPS - j) for j in range(SWEEPS + 1)]

    await_bytes(fwin.at[:, :, pl.ds(SUB, inner)], f_sem.at[1])
    loop(0, owned, scale_in)
    for j in range(1, SWEEPS + 1):
        run(j, 0, ready[j], early[j])
    await_bytes(fwin.at[:, :, pl.ds(SUB, nx - inner)], f_sem.at[2])
    loop(owned, groups, scale_in)
    for j in range(1, SWEEPS + 1):
        run(j, ready[j], owned, need[j])

    row = jnp.zeros((1, LANES), jnp.float32)
    lane1 = lax.broadcasted_iota(jnp.int32, (1, LANES), 1)
    for j, m in enumerate(moments):
        value = jnp.sum(jnp.sum(m, axis=0, keepdims=True), axis=1, keepdims=True)
        row = jnp.where(lane1 == j, value, row)
    part[...] = row
    red[me] = row
    peers(lambda dt, ds: r_copy(dt, ds).start())

    def scaled(l, t, it, begin):
        i = l + half * spare

        def get(c):
            q = qs[it, t, c, at(i), :]
            return scl[c, at(i), :] * q if begin else q

        def put(c, x):
            qs[it, t, c, at(i), :] = x
        return get, put

    def unweave(swap, begin):
        loop(0, owned, lambda l: [
            swap([scaled(l, t, it, begin) for t in range(steps)]) for it in range(ITERS)] and None)

    interleave(unweave)
    await_bytes(red.at[pl.ds(0, n - 1)], r_sem.at[1])
    total = lax.fori_loop(0, n, lambda j, acc: acc + red[j], jnp.zeros((1, LANES), jnp.float32))
    n1, n2, n3, n4, n5, n6 = [
        jnp.sum(jnp.where(lane1 == j, total, 0.0), axis=1, keepdims=True) for j in range(6)]

    tiny = 1e-7
    d1 = jnp.maximum(n2, 1e-37)
    l21, l31 = n3 / d1, n4 / d1
    d2 = jnp.maximum(n4 - l21 * n3, jnp.maximum(tiny * n4, 1e-37))
    e32 = n5 - l31 * n3
    l32 = e32 / d2
    d3 = jnp.maximum(n6 - l31 * n4 - l32 * e32, jnp.maximum(tiny * n6, 1e-37))
    y2 = n2 - l21 * n1
    y3 = n3 - l31 * n1 - l32 * y2
    a2 = y3 / d3
    a1 = y2 / d2 - l32 * a2
    a0 = n1 / d1 - l21 * a1 - l31 * a2

    def finish(l):
        i = l + half * spare
        for c in range(own):
            for t in range(steps):
                res[t, c, flat(l), :] = (
                    a0 * qs[0, t, c, at(i), :] + a1 * qs[1, t, c, at(i), :]
                    + a2 * qs[2, t, c, at(i), :])

    own_out = pltpu.make_async_copy(
        res_piece(mt, ml), out_hbm.at[:, pl.ds(mb * own, own)], o_sem.at[1])
    for i in range(strips):
        dl = home(i)
        for r in range(rows // SUB):
            finish(dl * (rows // SUB) + r)
        for jt in range(ntm):
            if (i, jt) == (strips - 2, 0):
                own_out.start()
            else:
                o_copy(turn(mt, jt, ntm), dl).start()
    await_bytes(kstage.at[pl.ds(0, strips - 1)], k_sem.at[0])
    await_bytes(fstage.at[:, pl.ds(0, nb - 1)], f_sem.at[0])

    @pl.when(edge)
    def _():
        await_bytes(kstage, k_sem.at[0])
        await_bytes(fstage, f_sem.at[0])

    await_bytes(red.at[pl.ds(0, n - 1)], r_sem.at[0])
    await_bytes(out_hbm, o_sem.at[1])
    await_bytes(out_hbm.at[:, pl.ds(0, (nb - 1) * own)], o_sem.at[0])


def solution(mesh):
    ntm, nsp = mesh.shape["tm"], mesh.shape["space"]
    n, nb = ntm * nsp, ntm * (nsp // 2)

    def body(forcing, conductivity):
        tl, rows, columns = forcing.shape
        tiles = columns // LANES
        own = tiles // nb
        width = own + 1
        reach = -(-(SWEEPS + 1) // rows)
        steps, nx = tl * ntm, (nsp // 2 + reach) * rows
        f = forcing.reshape(tl, rows, nb, own, LANES).transpose(0, 2, 3, 1, 4)
        k = conductivity.reshape(rows, nb, own, LANES).transpose(1, 2, 0, 3)
        padded = pltpu.VMEM((width, nx + 2 * SUB, LANES), jnp.float32)
        plain = pltpu.VMEM((width, nx, LANES), jnp.float32)

        def fields(*many):
            return pltpu.VMEM((*many, steps, width, nx + 2 * SUB, LANES), jnp.float32)

        dma = pltpu.SemaphoreType.DMA
        f, k = (pltpu.with_memory_space_constraint(x, pltpu.HBM) for x in (f, k))
        out = pl.pallas_call(
            functools.partial(kernel, ntm, nsp, reach),
            out_shape=jax.ShapeDtypeStruct((tl, tiles, rows, LANES), jnp.float32),
            in_specs=[pl.BlockSpec(memory_space=pltpu.HBM)] * 2,
            out_specs=pl.BlockSpec(memory_space=pl.ANY),
            scratch_shapes=[
                pltpu.VMEM((tl, nb, width, rows, LANES), jnp.float32),
                pltpu.VMEM((nb, own, rows, LANES), jnp.float32),
                pltpu.VMEM((nsp // 2, width, rows, LANES), jnp.float32),
                fields(), padded, padded, plain, plain, plain, plain, plain,
                fields(ITERS + 1), fields(ITERS), fields(ITERS), fields(ITERS), fields(),
                pltpu.VMEM((steps, own, nsp // 2 * rows, LANES), jnp.float32),
                pltpu.VMEM((1, LANES), jnp.float32),
                pltpu.VMEM((n, 1, LANES), jnp.float32),
                dma((3,)), dma((2,)), dma((2,)), dma((2,)), dma((3,)),
            ],
            compiler_params=pltpu.CompilerParams(
                collective_id=0, has_side_effects=True, vmem_limit_bytes=40 * 1024 * 1024),
        )(f, k)
        return out.transpose(0, 2, 1, 3).reshape(tl, rows, columns)

    return jax.shard_map(
        body,
        mesh=mesh,
        in_specs=(P("tm", "space", None), P("space", None)),
        out_specs=P("tm", "space", None),
        check_vma=False,
    )
```

time: 47.6 us -> 42.8 us (0.90)
  Pallas kernels: 46.6 us -> 41.9 us
    pallas_call x1, Pallas kernels: 46.6 us -> 41.9 us  [body(): pl.pallas_call(functools.partial(kernel, ntm, nsp, reach), out_shape=jax....]
where the time goes in v1:
time: 42.8 us; the launch traced here: 42.7 us
  Pallas kernels  41.9 us (98%)
  local copies, waits for them, and re-layouts  0.8 us (2%)
    pallas_call x1, Pallas kernels, body(): pl.pallas_call(functools.partial(kernel, ntm, nsp, reach), out_shape=jax....  41.9 us

profile of v1, /device:TPU:1, one launch (start us, length us, event | category | flops | bytes accessed | tf_op | source)
XLA Modules:
  0.0 42.7 jit_solution(5863114928579841987)
XLA Ops:
  0.0 41.9 %shard_map.28 = f32[1,128,8,128]{3,2,1,0:T(8,128)S(1)} custom-call(f32[1,16,8,8,128]{4,3,2,1,0:T(8,128)} %bitcast.10, f32[16,8,8,128]{3,2,1,0:T(8,128)} %bitcast.11), custom_call_target="tpu_custom_call" | custom-call | tf_op jit(solution)/shard_map/pallas_call | solution.py:491
  41.9 0.8 %copy.4 = f32[1,8,16384]{2,1,0:T(8,128)} copy(f32[1,8,16384]{2,1,0:T(8,128)S(1)} %bitcast.9) | data formatting | bytes 1048576

commit v2 on v1

--- a/solution.py
+++ b/solution.py
@@ -16,7 +16,7 @@
 
 def kernel(
     ntm, nsp, reach, f_hbm, k_hbm, out_hbm,
-    fstage, kloc, kstage, fwin, kwin, scl, inv, gn, gs, gw, ge, taus, abufs, bbufs, qs, last, res, part, red,
+    fstage, kloc, kstage, fwin, kwin, scl, inv, gn, gs, gw, ge, taus, abufs, bbufs, qs, last, ends, res, part, red,
     f_sem, k_sem, r_sem, o_sem, own_sem,
 ):
     n = ntm * nsp
@@ -236,14 +236,17 @@
         ends = turned(xs[0], xs[own - 1], xs[own])
         return [*xs[1:own], ends[2], ends[3]]
 
-    def near(i, offset):
-        return pl.ds(SUB + SUB * i + offset, SUB)
-
-    def at(i):
-        return pl.ds(pl.multiple_of(SUB + SUB * i, SUB), SUB)
-
-    def flat(i):
-        return pl.ds(pl.multiple_of(SUB * i, SUB), SUB)
+    def near(p, offset):
+        return pl.ds(SUB + p + offset, SUB)
+
+    def at(p):
+        return pl.ds(SUB + p, SUB)
+
+    def flat(p):
+        return pl.ds(p, SUB)
+
+    def by_group(act):
+        return lambda i: act(pl.multiple_of(SUB * i, SUB))
 
     inside = beside(mb, jnp.ones((SUB, LANES), jnp.float32), jnp.ones((SUB, LANES), jnp.float32))
 
@@ -267,46 +270,49 @@
             gw[c, flat(i), :] = half_s * (k + kl) * sl
             ge[c, flat(i), :] = half_s * (k + kr) * sr
 
-    loop(0, groups, weights_first)
-    loop(0, groups, weights_second)
-
-    def group(j):
-        return jnp.where(half == 0, j, groups - 1 - j)
+    loop(0, groups, by_group(weights_first))
+    loop(0, groups, by_group(weights_second))
+
+    def start_of(row):
+        return jnp.where(half == 0, row, nx - SUB - row)
+
+    down_rows = lax.broadcasted_iota(jnp.int32, (SUB, LANES), 0)
+    inwards = jnp.where(half == 0, down_rows, SUB - 1 - down_rows)
 
     def scale_in(j):
-        i = group(j)
+        i = pl.multiple_of(start_of(SUB * j), SUB)
         for c in range(width):
             s = scl[c, at(i), :]
             for t in range(steps):
                 taus[0, t, c, at(i), :] = s * fwin[steps - 1 - t, c, at(i), :]
 
-    def sweep(src, use, low, high, total):
-        def block(j, total):
-            i = group(j)
-            ends = []
-            for t in range(steps):
-                ends.append(turned(src[t, 0, at(i), :], src[t, own - 1, at(i), :], src[t, own, at(i), :]))
-
-            def beside_of(t, c):
-                here = ends[t]
-                left = here[0] if c == 0 else here[1] if c == own else src[t, c - 1, at(i), :]
-                right = here[2] if c == own - 1 else here[3] if c == own else src[t, c + 1, at(i), :]
-                return left, right
-
-            for c in (*range(1, own - 1), 0, own - 1, own):
+    def turn_ends(src, firsts):
+        for j, row in enumerate(firsts):
+            i = start_of(row)
+            for t in range(steps):
+                cells = turned(src[t, 0, at(i), :], src[t, own - 1, at(i), :], src[t, own, at(i), :])
+                for e, x in enumerate(cells):
+                    ends[j, t, e] = x
+
+    def sweep(src, use):
+        def block(j, row, total, counted):
+            i = start_of(row)
+            for c in range(width):
                 wn, wso = gn[c, flat(i), :], gs[c, flat(i), :]
                 ww, we = gw[c, flat(i), :], ge[c, flat(i), :]
                 out = []
                 for t in range(steps):
-                    left, right = beside_of(t, c)
+                    left = ends[j, t, 0] if c == 0 else ends[j, t, 1] if c == own else src[t, c - 1, at(i), :]
+                    right = (ends[j, t, 2] if c == own - 1 else ends[j, t, 3] if c == own
+                             else src[t, c + 1, at(i), :])
                     out.append(
                         wn * src[t, c, near(i, -1), :] + wso * src[t, c, near(i, 1), :]
                         + (ww * left + we * right))
                 term = use(c, i, [src[t, c, at(i), :] for t in range(steps)], out)
-                if term is not None and c < own:
-                    total = total + term
+                if term is not None and c < own and counted > 0:
+                    total = total + (term if counted >= SUB else jnp.where(inwards < counted, term, 0.0))
             return total
-        return lax.fori_loop(low, high, block, total)
+        return block
 
     def one(it):
         def use(c, i, x, g):
@@ -364,33 +370,31 @@
     plan += [(taus.at[ITERS], norm_one, 2 * ITERS - 1), (last, norm_two, 2 * ITERS - 1)]
     moments = [zero] * (2 * ITERS)
 
-    def run(number, low, middle, high):
+    def run(number, firsts, counted, looped=0):
         src, use, slot = plan[number - 1]
-        if low < middle:
-            base = zero if slot is None else moments[slot]
-            total = sweep(src, use, low, middle, base)
-            if slot is not None:
-                moments[slot] = total
-        if max(low, middle) < high:
-            sweep(src, use, max(low, middle), high, zero)
+        turn_ends(src, firsts)
+        block = sweep(src, use)
+        total = zero if slot is None else moments[slot]
+        if looped:
+            total = lax.fori_loop(0, looped, lambda j, acc: block(j, SUB * j, acc, SUB), total)
+        for j in range(looped, len(firsts)):
+            total = block(j, firsts[j], total, counted - SUB * j)
+        if slot is not None:
+            moments[slot] = total
 
     def up_to(count):
         return -(-count // SUB)
 
     inner = owned * SUB
-    ready = [(inner - j) // SUB for j in range(SWEEPS + 1)]
-    early = [max(up_to(SUB * ready[i] + i - j) for i in range(j, SWEEPS + 1))
-             for j in range(SWEEPS + 1)]
-    need = [owned + up_to(SWEEPS - j) for j in range(SWEEPS + 1)]
 
     await_bytes(fwin.at[:, :, pl.ds(SUB, inner)], f_sem.at[1])
     loop(0, owned, scale_in)
     for j in range(1, SWEEPS + 1):
-        run(j, 0, ready[j], early[j])
+        run(j, [SUB * i for i in range(up_to(inner - j))], inner - j, (inner - j) // SUB)
     await_bytes(fwin.at[:, :, pl.ds(SUB, nx - inner)], f_sem.at[2])
     loop(owned, groups, scale_in)
     for j in range(1, SWEEPS + 1):
-        run(j, ready[j], owned, need[j])
+        run(j, [inner - j + SUB * i for i in range(up_to(SWEEPS))], j)
 
     row = jnp.zeros((1, LANES), jnp.float32)
     lane1 = lax.broadcasted_iota(jnp.int32, (1, LANES), 1)
@@ -402,7 +406,7 @@
     peers(lambda dt, ds: r_copy(dt, ds).start())
 
     def scaled(l, t, it, begin):
-        i = l + half * spare
+        i = pl.multiple_of(SUB * (l + half * spare), SUB)
 
         def get(c):
             q = qs[it, t, c, at(i), :]
@@ -436,10 +440,10 @@
     a0 = n1 / d1 - l21 * a1 - l31 * a2
 
     def finish(l):
-        i = l + half * spare
+        i = pl.multiple_of(SUB * (l + half * spare), SUB)
         for c in range(own):
             for t in range(steps):
-                res[t, c, flat(l), :] = (
+                res[t, c, pl.ds(pl.multiple_of(SUB * l, SUB), SUB), :] = (
                     a0 * qs[0, t, c, at(i), :] + a1 * qs[1, t, c, at(i), :]
                     + a2 * qs[2, t, c, at(i), :])
 
@@ -499,6 +503,7 @@
                 pltpu.VMEM((nsp // 2, width, rows, LANES), jnp.float32),
                 fields(), padded, padded, plain, plain, plain, plain, plain,
                 fields(ITERS + 1), fields(ITERS), fields(ITERS), fields(ITERS), fields(),
+                pltpu.VMEM((nx // SUB, steps, 4, SUB, LANES), jnp.float32),
                 pltpu.VMEM((steps, own, nsp // 2 * rows, LANES), jnp.float32),
                 pltpu.VMEM((1, LANES), jnp.float32),
                 pltpu.VMEM((n, 1, LANES), jnp.float32),

time: 42.8 us -> 41.3 us (0.965)
  Pallas kernels: 41.9 us -> 40.4 us
    pallas_call x1, Pallas kernels: 41.9 us -> 40.4 us  [body(): pl.pallas_call(functools.partial(kernel, ntm, nsp, reach), out_shape=jax....]
where the time goes in v2:
time: 41.3 us; the launch traced here: 41.2 us
  Pallas kernels  40.4 us (98%)
  local copies, waits for them, and re-layouts  0.8 us (2%)
    pallas_call x1, Pallas kernels, body(): pl.pallas_call(functools.partial(kernel, ntm, nsp, reach), out_shape=jax....  40.4 us

profile of v2, /device:TPU:1, one launch (start us, length us, event | category | flops | bytes accessed | tf_op | source)
XLA Modules:
  0.0 41.2 jit_solution(2463246908443959161)
XLA Ops:
  0.0 40.4 %shard_map.28 = f32[1,128,8,128]{3,2,1,0:T(8,128)S(1)} custom-call(f32[1,16,8,8,128]{4,3,2,1,0:T(8,128)} %bitcast.10, f32[16,8,8,128]{3,2,1,0:T(8,128)} %bitcast.11), custom_call_target="tpu_custom_call" | custom-call | tf_op jit(solution)/shard_map/pallas_call | solution.py:495
  40.4 0.8 %copy.4 = f32[1,8,16384]{2,1,0:T(8,128)} copy(f32[1,8,16384]{2,1,0:T(8,128)S(1)} %bitcast.9) | data formatting | bytes 1048576
